TPU v7x, 256 devices: a whole 4x4x8 slice. The times are simulated.
256 devices in a mesh: bl: 64 (over y, z, core), ch: 4 (over x).
Axes of the slice: x: 4, y: 4, z: 8, core: 2. Of those that a mesh axis runs over, the one named last changes fastest.
Arguments:
- facet_grid: bfloat16 [4, 64, 16, 1024], P(None, None, None, 'ch'), may hold values from -0.75 to 0.75
- kernel: bfloat16 [131072, 1024], P('bl', 'ch'), may hold values from -0.1875 to 0.1875
- tile_of: int32 [256], P('bl'), may hold values from 0 to 3
- observed: bfloat16 [64, 2, 131072], P('ch', None, 'bl'), may hold values from -6 to 6
- flags: int32 [64, 131072], P('ch', 'bl'), may hold values 0 or 1
- pairs: int32 [2, 131072], P(None, 'bl'), may hold values from 0 to 511, as said below
- solver_order: int32 [512], replicated, may hold values from 0 to 511, as said below
Outputs:
- gains: float32 [64, 16, 512], P('ch', None, 'bl')
Inputs may be any that keep to these rules, and one draw needn't show every extreme that they name: `solver_order`: each station appears once. `pairs`: for row r, with j = (r mod 2048) // 32, the first station is solver_order[8 * j + m] for some m below 8; the second station differs from the first.
All inputs are finite; a program needn't handle non-finite values. No bound on the sum of `flags` on one device may be relied on, other than what follows from the above.
Results may differ from a plain program's by a relative error of at most 0.013.
Values may be sent and summed in bfloat16 or wider, within the bound.
No kernel may reach another device: no remote copies, remote signals or barrier semaphores. Data moves between devices by JAX's collectives and lax.ppermute only.
A program may use at most 128 MiB of HBM per device.

v0:
```python
import jax
import jax.numpy as jnp
from jax import lax
from jax.experimental import pallas as pl
from jax.experimental.pallas import tpu as pltpu
from jax.sharding import Mesh, PartitionSpec as P

S = 512
ITERS = 4
LANES = 128
ROWS = 2048
HALF = 512
CHUNK = 256
F32 = jnp.float32
BF16 = jnp.bfloat16
BL = ("y", "z", "core")
SMALL = pltpu.CompilerParams(vmem_limit_bytes=16 << 20)


def nt(a, b):
    return lax.dot_general(a, b, (((1,), (1,)), ((), ())), preferred_element_type=F32)


def nn(a, b):
    return lax.dot_general(a, b, (((1,), (0,)), ((), ())), preferred_element_type=F32)


def iota(shape, dim):
    return lax.broadcasted_iota(jnp.int32, shape, dim)


def lane_order():
    lane = iota((256, 256), 0)
    source = (lane & 15) * 16 + ((lane >> 4) & 7) * 2 + (lane >> 7)
    return (iota((256, 256), 1) == source).astype(F32).astype(BF16)


def in_hbm(x):
    return pltpu.with_memory_space_constraint(x, pltpu.HBM)


def full(shape):
    return pl.BlockSpec(shape, lambda i, *scalars: (0,) * len(shape))


def degrid_kernel(count):
    def run(where_ref, tile_ref, kern_ref, *refs):
        facets, outs, tables = refs[:count], refs[count : 3 * count], refs[3 * count : 4 * count]
        order = lane_order()
        for index in range(count):
            for tile in range(4):
                columns = slice(tile * 256, (tile + 1) * 256)
                tables[index][:, columns] = nn(order, facets[index][tile].reshape(256, 256)).astype(BF16)
        for block in range(4):
            rows = kern_ref[block * 16 : (block + 1) * 16].reshape(256, 256)
            place = slice((block % 2) * 256, (block % 2) * 256 + 256)
            columns = pl.ds(pl.multiple_of(tile_ref[block] * 256, 256), 256)
            for index in range(count):
                outs[2 * index + block // 2][place, :] = nt(rows, tables[index][:, columns]).astype(BF16)

    return run


def degrid(where, tile_of, kernel, facet_grid, groups):
    count = len(groups)

    def facet_spec(shift):
        return pl.BlockSpec((4, 16, 16, 256), lambda i, where, tile: (0, (where[0] + shift) & 3, 0, 0))

    half = jax.ShapeDtypeStruct((HALF, 256), BF16)
    table = pltpu.HBM((256, 1024), BF16)
    return pl.pallas_call(
        degrid_kernel(count),
        out_shape=[half] * (2 * count) + [table] * count,
        grid_spec=pltpu.PrefetchScalarGridSpec(
            num_scalar_prefetch=2,
            grid=(1,),
            in_specs=[full((64, 16, 256))] + [facet_spec(g) for g in groups],
            out_specs=[full((HALF, 256))] * (2 * count) + [full((256, 1024))] * count,
        ),
        compiler_params=SMALL,
    )(where, tile_of, in_hbm(kernel), *([in_hbm(facet_grid)] * count))


def late_kernel(jobs):
    def run(pay_ref, first_ref, second_ref, third_ref, *refs):
        outs, (lhs_ref, table_ref, sems) = refs[:-3], refs[-3:]
        loads = [
            pltpu.make_async_copy(source, table_ref.at[index], sems.at[index])
            for index, source in enumerate((first_ref, second_ref, third_ref))
        ]
        for load in loads:
            load.start()
        weight = (iota((LANES, 256), 0) == 52).astype(F32).astype(BF16)

        def mask(block, carry):
            segments = pl.ds(block * 16, 16)
            rows = pay_ref[segments, :16, :].reshape(256, 256)
            small = pay_ref[segments, 16:24, 128:].astype(F32).reshape(128, LANES)
            early = nn(small.astype(BF16), weight).reshape(16, 8, 256)
            late = nn(pltpu.roll(small, 64, 1).astype(BF16), weight).reshape(16, 8, 256)
            tile = jnp.concatenate([early, late], axis=1).reshape(256, 256)
            place = pl.ds(pl.multiple_of(block * 256, 256), 256)
            for t in range(4):
                lhs_ref[place, t * 256 : (t + 1) * 256] = rows * (tile == float(t)).astype(F32).astype(BF16)
            return carry

        lax.fori_loop(0, 4, mask, 0, unroll=2)
        for load in loads:
            load.wait()
        for half in range(2):
            for index, out, start in jobs[half]:
                source = lhs_ref[half * HALF : (half + 1) * HALF, :]
                outs[out][start : start + HALF, :] = nt(source, table_ref[index]).astype(BF16)

    return run


def late_degrid(payload, tables, jobs, shapes):
    vmem = pl.BlockSpec(memory_space=pltpu.VMEM)
    anywhere = pl.BlockSpec(memory_space=pl.ANY)
    return pl.pallas_call(
        late_kernel(jobs),
        out_shape=shapes,
        in_specs=[vmem, anywhere, anywhere, anywhere],
        out_specs=[vmem] * len(shapes),
        scratch_shapes=[
            pltpu.VMEM((1024, 1024), BF16),
            pltpu.VMEM((3, 256, 1024), BF16),
            pltpu.SemaphoreType.DMA((3,)),
        ],
        compiler_params=SMALL,
        name="late",
    )(payload, *[in_hbm(table) for table in tables])


def payload_kernel(tile_ref, obs_ref, flag_ref, pair_ref, kern_ref, out_ref, kept_ref, stacked_ref, sem):
    bulk = pltpu.make_async_copy(kern_ref.at[:, 16:32, :], out_ref.at[:, 0:16, :], sem)
    bulk.start()
    kept = (1 - flag_ref[...]).astype(F32)
    pair = pair_ref[...]
    high = (pair >> 3).astype(F32)
    low = (pair & 7).astype(F32)
    block = iota((1, ROWS), 1) >> 9
    tile = jnp.where(block < 2, jnp.where(block == 0, tile_ref[0], tile_ref[1]), jnp.where(block == 2, tile_ref[2], tile_ref[3]))
    fill = jnp.zeros((64 - 53, ROWS), F32)
    obs = obs_ref[...].astype(F32)
    stacked_ref[...] = jnp.concatenate([obs[:, 0], obs[:, 1], kept, high, low, tile.astype(F32), fill], axis=0)
    source = iota((64, 256), 0)
    col = iota((64, 256), 1)
    pick = (source == 32 + (col & 15)) & ((col < 32) | (col >= 128))
    pick = pick.astype(F32).astype(BF16)
    rest = (iota((LANES, LANES), 1) >= 32).astype(F32)

    def step(part, carry):
        turned = stacked_ref[:, pl.ds(pl.multiple_of(part * 128, 128), 128)].T
        wide = nn(turned.astype(BF16), pick)
        turned = jnp.concatenate([turned, jnp.zeros((128, 64), F32)], axis=1)
        value = turned * (wide[:, :128] + rest)
        moved = pltpu.roll(value, 64, 1).reshape(4, 4, 8, LANES)
        value = value.reshape(4, 4, 8, LANES)
        segments = pl.ds(part * 4, 4)
        out_ref[segments, 16:24, :128] = (value[:, 0] + moved[:, 1]).astype(BF16)
        out_ref[segments, 16:24, 128:] = (value[:, 2] + moved[:, 3]).astype(BF16)
        kept = wide[:, 128:].reshape(4, 32, LANES)[:, :16].reshape(64, LANES).astype(BF16)
        kept_ref[pl.ds(pl.multiple_of(part * 64, 64), 64), :] = kept
        return carry

    lax.fori_loop(0, ROWS // 128, step, 0, unroll=8)
    bulk.wait()


def make_payload(tile_of, observed, flags, pairs, kernel):
    return pl.pallas_call(
        payload_kernel,
        out_shape=[jax.ShapeDtypeStruct((64, 24, 256), BF16), jax.ShapeDtypeStruct((1024, LANES), BF16)],
        grid_spec=pltpu.PrefetchScalarGridSpec(
            num_scalar_prefetch=1,
            grid=(1,),
            in_specs=[
                full((16, 2, ROWS)),
                full((16, ROWS)),
                full((2, ROWS)),
                pl.BlockSpec(memory_space=pl.ANY),
            ],
            out_specs=[full((64, 24, 256)), full((1024, LANES))],
            scratch_shapes=[pltpu.VMEM((64, ROWS), F32), pltpu.SemaphoreType.DMA],
        ),
        compiler_params=SMALL,
        name="payload",
    )(tile_of, in_hbm(observed), in_hbm(flags), in_hbm(pairs), in_hbm(kernel))


def setup_kernel(pay_ref, order_ref, own_ref, ohq_ref, ohp_ref, opt_ref, vre_ref, vim_ref, kept_ref):
    source = iota((LANES, 5 * LANES), 0)
    col = iota((LANES, 5 * LANES), 1)
    piece = col >> 7
    weight = ((source == 16 * piece + (col & 15)) & (piece < 2)).astype(F32)
    weight = weight + 8.0 * ((source == 49) & (piece == 2)).astype(F32) + ((source == 51) & (piece == 2)).astype(F32)
    weight = weight + 8.0 * ((source == 48) & (piece == 3)).astype(F32) + ((source == 50) & (piece == 3)).astype(F32)
    weight = weight + ((source == 32 + (col & 15)) & (piece == 4)).astype(F32)
    weight = weight.astype(BF16)
    order = order_ref[...]
    own = own_ref[...]

    def step(i, carry):
        value = pay_ref[pl.ds(pl.multiple_of(i * 8, 8), 8), 16:24, :].astype(F32).reshape(64, 256)
        left, right = value[:, :128], value[:, 128:]
        value = jnp.concatenate([left, pltpu.roll(left, 64, 1), right, pltpu.roll(right, 64, 1)], axis=0)
        wide = nn(value.astype(BF16), weight).reshape(4, 8, 8, 5 * LANES)
        for part in range(2):
            rows = pl.ds(pl.multiple_of(i * 128 + part * 1024, 128), 128)
            mine = jnp.concatenate([wide[2 * part], wide[2 * part + 1]], axis=1).reshape(128, 5 * LANES)
            vre_ref[rows, :] = mine[:, :128].astype(BF16)
            vim_ref[rows, :] = mine[:, 128:256].astype(BF16)
            second = mine[:, 256:384]
            for quarter in range(4):
                lanes = slice(quarter * 128, (quarter + 1) * 128)
                ohq_ref[rows, lanes] = (second == order[:, lanes]).astype(F32).astype(BF16)
            near = (mine[:, 384:512] == own).astype(F32)
            ohp_ref[rows, :] = near.astype(BF16)
            opt_ref[:, rows] = near.T[:16, :].astype(BF16)
            if part == 1:
                kept_ref[pl.ds(pl.multiple_of(i * 128, 128), 128), :] = mine[:, 512:].astype(BF16)
        return carry

    lax.fori_loop(0, 8, step, 0)


def make_setup(payload, order, own):
    shapes = [
        pltpu.HBM((ROWS, S), BF16),
        pltpu.HBM((ROWS, LANES), BF16),
        jax.ShapeDtypeStruct((16, ROWS), BF16),
        jax.ShapeDtypeStruct((ROWS, LANES), BF16),
        jax.ShapeDtypeStruct((ROWS, LANES), BF16),
        pltpu.HBM((1024, LANES), BF16),
    ]
    return pl.pallas_call(setup_kernel, out_shape=shapes, compiler_params=SMALL, name="setup")(payload, order, own)


def over_directions(x):
    x = x + pltpu.roll(x, 16, 1)
    x = x + pltpu.roll(x, 32, 1)
    return x + pltpu.roll(x, 64, 1)


def iterate_kernel(first):
    def run(*refs):
        if first:
            model_a, chain_a, chain_b, opt_ref, vre_ref, vim_ref, *sources = refs[:11]
            out_ref, model_b, terms_ref, kept_ref, own_a, own_b, near_a, near_b, sems = refs[11:]
            kept_source, a_source, b_source, low_source, high_source = sources
            moves = [
                (kept_source, kept_ref),
                (a_source, own_a),
                (b_source, own_b),
                (high_source.at[HALF:], near_a),
                (low_source.at[HALF:], near_b),
            ]
            moves = [pltpu.make_async_copy(*move, sems.at[index]) for index, move in enumerate(moves)]
            for move in moves:
                move.start()
        else:
            model_a, model_b, opt_ref, vre_ref, vim_ref, ohq_ref, ohp_ref, here_ref, there_ref, own_ref, out_ref, terms_ref = refs
            all_gains = jnp.concatenate([here_ref[...], there_ref[...]], axis=0)
            own = own_ref[...]
            high = own.astype(BF16).astype(F32)
            near_gains = jnp.concatenate([high, own - high, jnp.zeros((LANES - 16, 256), F32)], axis=0).astype(BF16)

        for i in range(ROWS // CHUNK):
            if first and i == 4:
                for move in moves:
                    move.wait()
                add_kernel(own_a, own_b, chain_a, chain_b, near_a, near_b, kept_ref, model_b)
            rows = slice(i * CHUNK, (i + 1) * CHUNK)
            model = (model_a if i < 4 else model_b)[(i % 4) * CHUNK : (i % 4 + 1) * CHUNK, :].astype(F32)
            model_re, model_im = model[:, :128], model[:, 128:]
            if first:
                prod_re = pred_re = model_re
                prod_im = pred_im = model_im
            else:
                far = nn(ohq_ref[rows, :], all_gains)
                near = nn(ohp_ref[rows, :], near_gains)
                far_re, far_im = far[:, :128], far[:, 128:]
                near_re, near_im = near[:, :128], near[:, 128:]
                prod_re = model_re * far_re + model_im * far_im
                prod_im = model_im * far_re - model_re * far_im
                pred_re = near_re * prod_re - near_im * prod_im
                pred_im = near_re * prod_im + near_im * prod_re
            res_re = vre_ref[rows, :].astype(F32) - over_directions(pred_re)
            res_im = vim_ref[rows, :].astype(F32) - over_directions(pred_im)
            terms = jnp.concatenate(
                [
                    prod_re * res_re + prod_im * res_im,
                    prod_re * res_im - prod_im * res_re,
                    prod_re * prod_re + prod_im * prod_im,
                ],
                axis=1,
            )
            top = terms.astype(BF16)
            terms_ref[rows, :384] = top
            terms_ref[rows, 384:] = (terms - top.astype(F32)).astype(BF16)

        acc = nn(opt_ref[...], terms_ref[...])[:8]
        acc = acc[:, :384] + acc[:, 384:]
        sum_re, sum_im, power = acc[:, :128], acc[:, 128:256], acc[:, 256:]
        if first:
            gain_re = jnp.ones((8, 128), F32)
            gain_im = jnp.zeros((8, 128), F32)
        else:
            gain_re, gain_im = own[:, :128], own[:, 128:]
        new_re = (sum_re + gain_re * power) / (power + 1.0)
        new_im = (sum_im + gain_im * power) / (power + 1.0)
        out_ref[:, :128] = (gain_re + new_re) * 0.5
        out_ref[:, 128:] = (gain_im + new_im) * 0.5

    return run


def iterate(args, first):
    vmem = pl.BlockSpec(memory_space=pltpu.VMEM)
    anywhere = pl.BlockSpec(memory_space=pl.ANY)
    scratch = [pltpu.VMEM((ROWS, 768), BF16)]
    if first:
        scratch += [pltpu.VMEM((1024, LANES), BF16)]
        scratch += [pltpu.VMEM((HALF, 256), BF16)] * 4 + [pltpu.SemaphoreType.DMA((5,))]
    return pl.pallas_call(
        iterate_kernel(first),
        out_shape=[jax.ShapeDtypeStruct((8, 256), F32)] + [jax.ShapeDtypeStruct((1024, 256), BF16)] * first,
        in_specs=[vmem] * 6 + [anywhere] * 5 if first else [vmem] * len(args),
        out_specs=[vmem] * (2 if first else 1),
        scratch_shapes=scratch,
        compiler_params=SMALL,
        name="iterate0" if first else "iterate",
    )(*args)


def smooth_kernel(last):
    def run(where_ref, mid_ref, low_ref, high_ref, *outs):
        chan = iota((8, LANES), 1) & 15
        whole = chan + 16 * where_ref[0]
        has_left = (whole > 0).astype(F32)
        has_right = (whole < 63).astype(F32)
        halves = []
        for part in range(2):
            lanes = slice(part * 128, (part + 1) * 128)
            mid = mid_ref[:, lanes]
            left = jnp.where(chan == 0, pltpu.roll(low_ref[:, lanes], 113, 1), pltpu.roll(mid, 1, 1))
            right = jnp.where(chan == 15, pltpu.roll(high_ref[:, lanes], 15, 1), pltpu.roll(mid, 127, 1))
            total = 0.25 * has_left * left + 0.5 * mid + 0.25 * has_right * right
            halves.append(total / (0.5 + 0.25 * has_left + 0.25 * has_right))
        gains = jnp.concatenate(halves, axis=1)
        if last:
            source = iota((256, 256), 0)
            place = (source & 15) * 16 + ((source >> 4) & 7) * 2 + (source >> 7)
            order = (iota((256, 256), 1) == place).astype(F32)
            gains = jnp.dot(gains, order, precision=lax.Precision.HIGHEST, preferred_element_type=F32)
            for channel in range(16):
                outs[0][channel] = gains[:, channel * 16 : (channel + 1) * 16]
        else:
            outs[0][...] = gains
            outs[1][...] = jnp.broadcast_to(gains.astype(BF16)[None], (32, 8, 256))

    return run


def smooth(where, mid, low, high, last):
    if last:
        shapes = [jax.ShapeDtypeStruct((16, 8, 16), F32)]
    else:
        shapes = [jax.ShapeDtypeStruct((8, 256), F32), jax.ShapeDtypeStruct((32, 8, 256), BF16)]
    smem = pl.BlockSpec(memory_space=pltpu.SMEM)
    vmem = pl.BlockSpec(memory_space=pltpu.VMEM)
    return pl.pallas_call(
        smooth_kernel(last),
        out_shape=shapes,
        in_specs=[smem, vmem, vmem, vmem],
        out_specs=[vmem] * len(shapes),
        compiler_params=SMALL,
        name="finish" if last else "smooth",
    )(where, mid, low, high)


def pair_kernel(left_ref, right_ref, out_ref):
    for part in range(2):
        rows = slice(part * 256, (part + 1) * 256)
        out_ref[rows, :] = (left_ref[rows, :].astype(F32) + right_ref[rows, :].astype(F32)).astype(BF16)


def pair_sum(left, right):
    block = pl.BlockSpec((HALF, 256), lambda i: (0, 0))
    return pl.pallas_call(
        pair_kernel,
        out_shape=jax.ShapeDtypeStruct((HALF, 256), BF16),
        grid=(1,),
        in_specs=[block, block],
        out_specs=block,
        compiler_params=SMALL,
        name="pair",
    )(in_hbm(left) if left.shape[0] > HALF else left, right)


def add_kernel(own_a, own_b, chain_a, chain_b, near_a, near_b, kept_ref, out_ref):
    for half, parts in ((0, (own_a, chain_a, near_a)), (1, (own_b, chain_b, near_b))):
        for part in range(2):
            near = slice(part * 256, (part + 1) * 256)
            rows = slice(half * HALF + part * 256, half * HALF + (part + 1) * 256)
            total = parts[0][near, :].astype(F32) + parts[1][near, :].astype(F32) + parts[2][near, :].astype(F32)
            kept = kept_ref[rows, :].astype(F32)
            out_ref[rows, :128] = (total[:, :128] * kept).astype(BF16)
            out_ref[rows, 128:] = (total[:, 128:] * kept).astype(BF16)


def total(*parts):
    return pl.pallas_call(
        add_kernel, out_shape=jax.ShapeDtypeStruct((1024, 256), BF16), compiler_params=SMALL, name="add"
    )(*parts)


UP = [(i, (i + 1) % 4) for i in range(4)]
DOWN = [(i, (i + 3) % 4) for i in range(4)]


def last_legs(chain_a, chain_b, direct_a, direct_b, next_a, prev_b):
    chain_a = lax.ppermute(pair_sum(chain_a, next_a), "ch", UP)
    chain_b = lax.ppermute(pair_sum(chain_b, prev_b), "ch", DOWN)
    return chain_a, chain_b, direct_a, direct_b


def exchange(value):
    return lax.all_to_all(value, BL, split_axis=0, concat_axis=0, tiled=True)


def body(facet_grid, kernel, tile_of, observed, flags, pairs, solver_order):
    where = lax.axis_index("ch").astype(jnp.int32).reshape(1)
    tile_of = in_hbm(tile_of)
    kernel = kernel.reshape(64, 32, 256)
    payload, kept_a = make_payload(tile_of, observed, flags, pairs, kernel)
    arrived = exchange(payload)

    mine = lax.dynamic_slice(solver_order, (8 * lax.axis_index(BL),), (8,))
    own_row = jnp.concatenate([mine, mine, jnp.full((LANES - 16,), -1, jnp.int32)]).astype(F32).reshape(1, LANES)
    halves = solver_order.reshape(32, 2, 8).transpose(1, 0, 2).astype(F32).reshape(2, S // 2)
    order_row = jnp.where(lax.axis_index("core") == 0, halves, halves[::-1]).reshape(1, S)

    far_a, far_b, table2 = degrid(where, tile_of, kernel, facet_grid, (2,))
    chain_a = lax.ppermute(far_a, "ch", UP)
    chain_b = lax.ppermute(far_b, "ch", DOWN)
    next_a, next_b, prev_a, prev_b, own_a, own_b, table1, table3, table0 = degrid(
        where, tile_of, kernel, facet_grid, (1, 3, 0)
    )
    direct_a = lax.ppermute(prev_a, "ch", DOWN)
    direct_b = lax.ppermute(next_b, "ch", UP)
    legs = last_legs(chain_a, chain_b, direct_a, direct_b, next_a, prev_b)
    model_a = total(own_a, own_b, *legs, kept_a)

    half = jax.ShapeDtypeStruct((HALF, 256), BF16)
    away = pltpu.HBM((HALF, 256), BF16)
    whole = pltpu.HBM((2 * HALF, 256), BF16)
    going_up, going_down = late_degrid(
        arrived,
        (table2, table3, table1),
        (((0, 0, 0), (1, 1, HALF)), ((0, 1, 0), (2, 0, HALF))),
        [whole, whole],
    )
    from_low = lax.ppermute(going_up, "ch", UP)
    from_high = lax.ppermute(going_down, "ch", DOWN)
    next_a, prev_b, own_a, own_b = late_degrid(
        arrived, (table1, table3, table0), (((0, 0, 0), (2, 2, 0)), ((1, 1, 0), (2, 3, 0))), [half, half, away, away]
    )
    ohq, ohp, opt, vis_re, vis_im, kept_b = make_setup(arrived, order_row, own_row)
    chain_a, chain_b, *_ = last_legs(from_low, from_high, None, None, next_a, prev_b)
    model_a = exchange(model_a.reshape(64, 16, 256)).reshape(1024, 256)

    for step in range(ITERS):
        if step == 0:
            sources = map(in_hbm, (kept_b, own_a, own_b, from_low, from_high))
            mid, model_b = iterate((model_a, chain_a, chain_b, opt, vis_re, vis_im, *sources), True)
        else:
            rows = (model_a, model_b, opt, vis_re, vis_im, ohq, ohp)
            both = (everyone.reshape(S // 2, 256), others.reshape(S // 2, 256))
            (mid,) = iterate(rows + both + (gains,), False)
        low = lax.ppermute(mid, "ch", UP)
        high = lax.ppermute(mid, "ch", DOWN)
        if step + 1 < ITERS:
            gains, block = smooth(where, mid, low, high, False)
            everyone = lax.all_to_all(block, ("y", "z"), split_axis=0, concat_axis=0, tiled=True)
            others = lax.ppermute(everyone, "core", [(0, 1), (1, 0)])
        else:
            (gains,) = smooth(where, mid, low, high, True)
    return gains.transpose(0, 2, 1)


def solution(mesh):
    split = Mesh(mesh.devices.reshape(4, 8, 2, 4), BL + ("ch",))
    in_specs = (
        P(None, None, None, "ch"),
        P(BL, "ch"),
        P(BL),
        P("ch", None, BL),
        P("ch", BL),
        P(None, BL),
        P(),
    )
    out_specs = P("ch", None, BL)
    return jax.shard_map(body, mesh=split, in_specs=in_specs, out_specs=out_specs, check_vma=False)
```

profile of v0, /device:TPU:1, one launch (start us, length us, event | category | flops | bytes accessed | tf_op | source)
XLA Modules:
  0.0 172.8 jit_solution(8380874955065214869)
XLA Ops:
  0.0 3.6 %payload.1 = (bf16[64,24,256]{2,1,0:T(8,128)(2,1)}, bf16[1024,128]{1,0:T(8,128)(2,1)S(1)}) custom-call(s32[4]{0:T(128)} %tile_ref.5, bf16[16,2,2048]{2,1,0:T(2,128)(2,1)} %obs_ref.1, s32[16,2048]{1,0:T(8,128)} %flag_ref.1, s32[2,2048]{1,0:T(2,128)} %pair_ref.1, bf16[64,32,256]{2,1,0:T(8,128)(2,1)} %bitcast.33), custom_call_target="tpu_custom_call" | custom-call | tf_op jit(solution)/shard_map/payload/pallas_call | solution.py:174
  3.6 13.2 %all-to-all-start.1 = ((bf16[64,24,256]{2,1,0:T(8,128)(2,1)}), bf16[64,24,256]{2,1,0:T(8,128)(2,1)S(1)}, u32[]{:S(2)}, u32[]{:S(2)}) async-start(bf16[64,24,256]{2,1,0:T(8,128)(2,1)} %get-tuple-element.48), calls=%async_computation.1 | async-start | bytes 1572864 | tf_op jit(solution)/shard_map/all_to_all | solution.py:432
  16.7 3.0 %shard_map.74 = (bf16[512,256]{1,0:T(8,128)(2,1)S(1)}, bf16[512,256]{1,0:T(8,128)(2,1)S(1)}, bf16[256,1024]{1,0:T(8,128)(2,1)}) custom-call(s32[1]{0:T(128)} %bitcast.where_ref, s32[4]{0:T(128)} %tile_ref.5, bf16[64,32,256]{2,1,0:T(8,128)(2,1)} %bitcast.34, bf16[4,64,16,256]{3,2,1,0:T(8,128)(2,1)} %refs_0_.3), custom_call_target="tpu_custom_call" | custom-call | tf_op jit(solution)/shard_map/pallas_call | solution.py:72
  19.7 1.2 collective-permute-start
  21.0 1.5 collective-permute-start.2
  22.4 4.2 %shard_map.73 = (bf16[512,256]{1,0:T(8,128)(2,1)S(1)}, bf16[512,256]{1,0:T(8,128)(2,1)S(1)}, bf16[512,256]{1,0:T(8,128)(2,1)S(1)}, bf16[512,256]{1,0:T(8,128)(2,...) custom-call(s32[1]{0:T(128)} %bitcast.where_ref, ...), custom_call_target="tpu_custom_call" | custom-call | tf_op jit(solution)/shard_map/pallas_call | solution.py:72
  26.6 1.3 collective-permute-start.4
  28.6 2.7 %collective-permute-start.3 = (bf16[512,256]{1,0:T(8,128)(2,1)S(1)}, bf16[512,256]{1,0:T(8,128)(2,1)S(1)}, u32[]{:S(2)}, u32[]{:S(2)}) collective-permute-start(bf16[512,256]{1,0:T(8,128)(2,1)S(1)} %pair.5), channel_id=1, source_target_pairs={{0,3},{1,0},{2,1},{3,2},{4,7},{5,4},{6,5},{7,6},{8,11},{9,8},{10,9... | collective-permute-start | bytes 786440 | tf_op jit(solution)/shard_map/ppermute | solution.py:427
  31.3 2.1 %collective-permute-done.4.near_a = bf16[512,256]{1,0:T(8,128)(2,1)S(1)} collective-permute-done((bf16[512,256]{1,0:T(8,128)(2,1)S(1)}, bf16[512,256]{1,0:T(8,128)(2,1)S(1)}, u32[]{:S(2)}, u32[]{:S(2)}) %collective-permute-start.4) | collective-permute-done | bytes 262176 | tf_op jit(solution)/shard_map/ppermute | solution.py:453
  33.5 2.2 %collective-permute-done.5.near_b = bf16[512,256]{1,0:T(8,128)(2,1)S(1)} collective-permute-done((bf16[512,256]{1,0:T(8,128)(2,1)S(1)}, bf16[512,256]{1,0:T(8,128)(2,1)S(1)}, u32[]{:S(2)}, u32[]{:S(2)}) %collective-permute-start.5) | collective-permute-done | bytes 262176 | tf_op jit(solution)/shard_map/ppermute | solution.py:454
  35.7 5.6 %collective-permute-done.1.chain_a = bf16[512,256]{1,0:T(8,128)(2,1)S(1)} collective-permute-done((bf16[512,256]{1,0:T(8,128)(2,1)S(1)}, bf16[512,256]{1,0:T(8,128)(2,1)S(1)}, u32[]{:S(2)}, u32[]{:S(2)}) %collective-permute-start.1) | collective-permute-done | bytes 262176 | tf_op jit(solution)/shard_map/ppermute | solution.py:426
  41.3 1.1 add.19
  42.4 12.2 %all-to-all-start = ((bf16[64,16,256]{2,1,0:T(8,128)(2,1)}), bf16[64,16,256]{2,1,0:T(8,128)(2,1)S(1)}, u32[]{:S(2)}, u32[]{:S(2)}) async-start(bf16[64,16,256]{2,1,0:T(8,128)(2,1)} %bitcast.2), calls=%async_computation | async-start | bytes 1048576 | tf_op jit(solution)/shard_map/all_to_all | solution.py:432
  54.6 3.7 %late.2 = (bf16[1024,256]{1,0:T(8,128)(2,1)}, bf16[1024,256]{1,0:T(8,128)(2,1)}) custom-call(bf16[64,24,256]{2,1,0:T(8,128)(2,1)S(1)} %all-to-all-done.1.pay_ref, bf16[256,1024]{1,0:T(8,128)(2,1)} %get-tuple-element.49.first_ref, bf16[256,1024]{1,0:T(8,128)(2,1)} %get-tuple-element.50.second_ref, bf16[256,1024]{1,0:T(8,128)(2,1)} %get-tuple-element.51.third_ref.first_ref), custom_call_target="tpu_custom_call" | custom-call | tf_op jit(solution)/shard_map/late/pallas_call | solution.py:122
  58.4 2.7 %collective-permute-start.8 = (bf16[1024,256]{1,0:T(8,128)(2,1)}, bf16[1024,256]{1,0:T(8,128)(2,1)S(1)}, u32[]{:S(2)}, u32[]{:S(2)}) collective-permute-start(bf16[1024,256]{1,0:T(8,128)(2,1)} %get-tuple-element.55), channel_id=1, source_target_pairs={{0,3},{1,0},{2,1},{3,2},{4,7},{5,4},{6,5},{7,6},{8,11},{9,8},{10,9... | collective-permute-start | bytes 1572872 | tf_op jit(solution)/shard_map/ppermute | solution.py:468
  61.3 3.4 %late.3 = (bf16[512,256]{1,0:T(8,128)(2,1)S(1)}, bf16[512,256]{1,0:T(8,128)(2,1)S(1)}, bf16[512,256]{1,0:T(8,128)(2,1)}, bf16[512,256]{1,0:T(8,128)(2,1)}) custom-call(bf16[64,24,256]{2,1,0:T(8,128)(2,1)S(1)} %all-to-all-done.1.pay_ref, bf16[256,1024]{1,0:T(8,128)(2,1)} %get-tuple-element.51.third_ref.first_ref, ...), custom_call_target="tpu_custom_call" | custom-call | tf_op jit(solution)/shard_map/late/pallas_call | solution.py:122
  64.7 8.1 %collective-permute-done.6.left_ref.refs_9_ = bf16[1024,256]{1,0:T(8,128)(2,1)S(1)} collective-permute-done((bf16[1024,256]{1,0:T(8,128)(2,1)}, bf16[1024,256]{1,0:T(8,128)(2,1)S(1)}, u32[]{:S(2)}, u32[]{:S(2)}) %collective-permute-start.6) | collective-permute-done | bytes 524320 | tf_op jit(solution)/shard_map/ppermute | solution.py:467
  72.8 0.8 copy-done.2
  73.6 1.0 pair.6
  75.5 1.0 pair.7
  76.5 2.7 %collective-permute-start.9 = (bf16[512,256]{1,0:T(8,128)(2,1)S(1)}, bf16[512,256]{1,0:T(8,128)(2,1)S(1)}, u32[]{:S(2)}, u32[]{:S(2)}) collective-permute-start(bf16[512,256]{1,0:T(8,128)(2,1)S(1)} %pair.7), channel_id=1, source_target_pairs={{0,3},{1,0},{2,1},{3,2},{4,7},{5,4},{6,5},{7,6},{8,11},{9,8},{10,9... | collective-permute-start | bytes 786440 | tf_op jit(solution)/shard_map/ppermute | solution.py:427
  79.4 4.4 %setup.1 = (bf16[2048,512]{1,0:T(8,128)(2,1)}, bf16[2048,128]{1,0:T(8,128)(2,1)}, bf16[16,2048]{1,0:T(8,128)(2,1)S(1)}, bf16[2048,128]{1,0:T(8,128)(2,1)S(1)}, b...) custom-call(bf16[64,24,256]{2,1,0:T(8,128)(2,1)S(1)} %all-to-all-done.1.pay_ref, f32[1,512]{1,0:T(1,128)S(1)} %bitcast.32, ...), custom_call_target="tpu_custom_call" | custom-call | tf_op jit(solution)/shard_map/setup/pallas_call | solution.py:239
  83.8 3.1 %iterate0.1 = (f32[8,256]{1,0:T(8,128)S(1)}, bf16[1024,256]{1,0:T(8,128)(2,1)S(1)}) custom-call(bf16[1024,256]{1,0:T(8,128)(2,1)S(1)} %bitcast.22, bf16[512,256]{1,0:T(8,128)(2,1)S(1)} %collective-permute-done.7.refs_1_, bf16[512,256]{1,0:T(8,128)(2,1)S(1)} %collective-permute-done.9.refs_2_, bf16[16,2048]{1,0:T(8,128)(2,1)S(1)} %get-tuple-element.57.refs_3_.refs_2_, ...), custom_call_target="tpu_custom_call" | custom-call | tf_op jit(solution)/shard_map/iterate0/pallas_call | solution.py:328
  86.9 3.0 %collective-permute-start.11 = (f32[8,256]{1,0:T(8,128)S(1)}, f32[8,256]{1,0:T(8,128)S(1)}, u32[]{:S(2)}, u32[]{:S(2)}) collective-permute-start(f32[8,256]{1,0:T(8,128)S(1)} %get-tuple-element.66.mid_ref), channel_id=1, source_target_pairs={{0,3},{1,0},{2,1},{3,2},{4,7},{5,4},{6,5},{7,6},{8,11},{9,8},{10,9... | collective-permute-start | bytes 24584 | tf_op jit(solution)/shard_map/ppermute | solution.py:485
  89.9 0.8 collective-permute-done.11.high_ref
  90.6 2.9 %collective-permute-done.10.low_ref = f32[8,256]{1,0:T(8,128)S(1)} collective-permute-done((f32[8,256]{1,0:T(8,128)S(1)}, f32[8,256]{1,0:T(8,128)S(1)}, u32[]{:S(2)}, u32[]{:S(2)}) %collective-permute-start.10) | collective-permute-done | bytes 8224 | tf_op jit(solution)/shard_map/ppermute | solution.py:484
  93.7 18.6 %all_to_all.25 = bf16[32,8,256]{2,1,0:T(8,128)(2,1)S(1)} all-to-all(bf16[32,8,256]{2,1,0:T(8,128)(2,1)S(1)} %get-tuple-element.67), channel_id=1, replica_groups=mesh['y'=4,'z'=8,'core'=2,'ch'=4] {'y','z'}, dimensions={0} | all-to-all | bytes 262144 | tf_op jit(solution)/shard_map/all_to_all | solution.py:488
  112.2 5.2 %collective-permute-start.12 = (bf16[32,8,256]{2,1,0:T(8,128)(2,1)S(1)}, bf16[32,8,256]{2,1,0:T(8,128)(2,1)S(1)}, u32[]{:S(2)}, u32[]{:S(2)}) collective-permute-start(bf16[32,8,256]{2,1,0:T(8,128)(2,1)S(1)} %all_to_all.25), channel_id=1, source_target_pairs={{0,4},{4,0},{1,5},{5,1},{2,6},{6,2},{3,7},{7,3},{8,12},{12,8},{9,1... | collective-permute-start | bytes 393224 | tf_op jit(solution)/shard_map/ppermute | solution.py:489
  117.5 1.0 collective-permute-done.12
  118.5 2.9 %iterate.3.mid_ref = f32[8,256]{1,0:T(8,128)S(1)} custom-call(bf16[1024,256]{1,0:T(8,128)(2,1)S(1)} %bitcast.23, bf16[1024,256]{1,0:T(8,128)(2,1)S(1)} %get-tuple-element.63.refs_1_, bf16[16,2048]{1,0:T(8,128)(2,1)S(1)} %get-tuple-element.57.refs_3_.refs_2_, bf16[2048,128]{1,0:T(8,128)(2,1)S(1)} %get-tuple-element.58.refs_4_.refs_3_, ...), custom_call_target="tpu_custom_call" | custom-call | tf_op jit(solution)/shard_map/iterate/pallas_call | solution.py:328
  121.4 1.5 collective-permute-start.13
  122.9 1.0 collective-permute-done.14.high_ref
  123.9 1.5 collective-permute-done.13.low_ref
  125.5 12.5 %all_to_all.26 = bf16[32,8,256]{2,1,0:T(8,128)(2,1)S(1)} all-to-all(bf16[32,8,256]{2,1,0:T(8,128)(2,1)S(1)} %get-tuple-element.69), channel_id=1, replica_groups=mesh['y'=4,'z'=8,'core'=2,'ch'=4] {'y','z'}, dimensions={0} | all-to-all | bytes 262144 | tf_op jit(solution)/shard_map/all_to_all | solution.py:488
  138.0 2.9 %collective-permute-start.15 = (bf16[32,8,256]{2,1,0:T(8,128)(2,1)S(1)}, bf16[32,8,256]{2,1,0:T(8,128)(2,1)S(1)}, u32[]{:S(2)}, u32[]{:S(2)}) collective-permute-start(bf16[32,8,256]{2,1,0:T(8,128)(2,1)S(1)} %all_to_all.26), channel_id=1, source_target_pairs={{0,4},{4,0},{1,5},{5,1},{2,6},{6,2},{3,7},{7,3},{8,12},{12,8},{9,1... | collective-permute-start | bytes 393224 | tf_op jit(solution)/shard_map/ppermute | solution.py:489
  141.0 1.0 collective-permute-done.15
  142.0 2.9 %iterate.4.mid_ref = f32[8,256]{1,0:T(8,128)S(1)} custom-call(bf16[1024,256]{1,0:T(8,128)(2,1)S(1)} %bitcast.24, bf16[1024,256]{1,0:T(8,128)(2,1)S(1)} %get-tuple-element.63.refs_1_, bf16[16,2048]{1,0:T(8,128)(2,1)S(1)} %get-tuple-element.57.refs_3_.refs_2_, bf16[2048,128]{1,0:T(8,128)(2,1)S(1)} %get-tuple-element.58.refs_4_.refs_3_, ...), custom_call_target="tpu_custom_call" | custom-call | tf_op jit(solution)/shard_map/iterate/pallas_call | solution.py:328
  144.9 1.5 collective-permute-start.16
  146.4 1.0 collective-permute-done.17.high_ref
  147.4 1.3 collective-permute-done.16.low_ref
  148.8 12.4 %all_to_all.27 = bf16[32,8,256]{2,1,0:T(8,128)(2,1)S(1)} all-to-all(bf16[32,8,256]{2,1,0:T(8,128)(2,1)S(1)} %get-tuple-element.71), channel_id=1, replica_groups=mesh['y'=4,'z'=8,'core'=2,'ch'=4] {'y','z'}, dimensions={0} | all-to-all | bytes 262144 | tf_op jit(solution)/shard_map/all_to_all | solution.py:488
  161.2 2.9 %collective-permute-start.18 = (bf16[32,8,256]{2,1,0:T(8,128)(2,1)S(1)}, bf16[32,8,256]{2,1,0:T(8,128)(2,1)S(1)}, u32[]{:S(2)}, u32[]{:S(2)}) collective-permute-start(bf16[32,8,256]{2,1,0:T(8,128)(2,1)S(1)} %all_to_all.27), channel_id=1, source_target_pairs={{0,4},{4,0},{1,5},{5,1},{2,6},{6,2},{3,7},{7,3},{8,12},{12,8},{9,1... | collective-permute-start | bytes 393224 | tf_op jit(solution)/shard_map/ppermute | solution.py:489
  164.1 1.0 collective-permute-done.18
  165.1 2.9 %iterate.5.mid_ref = f32[8,256]{1,0:T(8,128)S(1)} custom-call(bf16[1024,256]{1,0:T(8,128)(2,1)S(1)} %bitcast.25, bf16[1024,256]{1,0:T(8,128)(2,1)S(1)} %get-tuple-element.63.refs_1_, bf16[16,2048]{1,0:T(8,128)(2,1)S(1)} %get-tuple-element.57.refs_3_.refs_2_, bf16[2048,128]{1,0:T(8,128)(2,1)S(1)} %get-tuple-element.58.refs_4_.refs_3_, ...), custom_call_target="tpu_custom_call" | custom-call | tf_op jit(solution)/shard_map/iterate/pallas_call | solution.py:328
  168.1 1.5 collective-permute-start.19
  169.6 1.0 collective-permute-done.20.high_ref
  170.6 1.3 collective-permute-done.19.low_ref
  171.9 1.0 finish.1
  (40 shorter events, 2.4 us)
Async XLA Ops:
  3.6 38.8 %all-to-all-start.1 = ((bf16[64,24,256]{2,1,0:T(8,128)(2,1)}), bf16[64,24,256]{2,1,0:T(8,128)(2,1)S(1)}, u32[]{:S(2)}, u32[]{:S(2)}) async-start(bf16[64,24,256]{2,1,0:T(8,128)(2,1)} %get-tuple-element.48), calls=%async_computation.1 | async-start | bytes 1572864 | tf_op jit(solution)/shard_map/all_to_all | solution.py:432
  19.7 8.6 %collective-permute-start = (bf16[512,256]{1,0:T(8,128)(2,1)S(1)}, bf16[512,256]{1,0:T(8,128)(2,1)S(1)}, u32[]{:S(2)}, u32[]{:S(2)}) collective-permute-start(bf16[512,256]{1,0:T(8,128)(2,1)S(1)} %get-tuple-element.41), channel_id=1, source_target_pairs={{0,1},{1,2},{2,3},{3,0},{4,5},{5,6},{6,7},{7,4},{8,9},{9,10},{10,1... | collective-permute-start | bytes 786440 | tf_op jit(solution)/shard_map/ppermute | solution.py:448
  21.0 7.6 %collective-permute-start.2 = (bf16[512,256]{1,0:T(8,128)(2,1)S(1)}, bf16[512,256]{1,0:T(8,128)(2,1)S(1)}, u32[]{:S(2)}, u32[]{:S(2)}) collective-permute-start(bf16[512,256]{1,0:T(8,128)(2,1)S(1)} %get-tuple-element.43), channel_id=1, source_target_pairs={{0,3},{1,0},{2,1},{3,2},{4,7},{5,4},{6,5},{7,6},{8,11},{9,8},{10,9... | collective-permute-start | bytes 786440 | tf_op jit(solution)/shard_map/ppermute | solution.py:449
  26.6 6.9 %collective-permute-start.4 = (bf16[512,256]{1,0:T(8,128)(2,1)S(1)}, bf16[512,256]{1,0:T(8,128)(2,1)S(1)}, u32[]{:S(2)}, u32[]{:S(2)}) collective-permute-start(bf16[512,256]{1,0:T(8,128)(2,1)S(1)} %get-tuple-element.45), channel_id=1, source_target_pairs={{0,3},{1,0},{2,1},{3,2},{4,7},{5,4},{6,5},{7,6},{8,11},{9,8},{10,9... | collective-permute-start | bytes 786440 | tf_op jit(solution)/shard_map/ppermute | solution.py:453
  27.9 7.8 %collective-permute-start.5 = (bf16[512,256]{1,0:T(8,128)(2,1)S(1)}, bf16[512,256]{1,0:T(8,128)(2,1)S(1)}, u32[]{:S(2)}, u32[]{:S(2)}) collective-permute-start(bf16[512,256]{1,0:T(8,128)(2,1)S(1)} %get-tuple-element.46), channel_id=1, source_target_pairs={{0,1},{1,2},{2,3},{3,0},{4,5},{5,6},{6,7},{7,4},{8,9},{9,10},{10,1... | collective-permute-start | bytes 786440 | tf_op jit(solution)/shard_map/ppermute | solution.py:454
  28.4 12.9 %collective-permute-start.1 = (bf16[512,256]{1,0:T(8,128)(2,1)S(1)}, bf16[512,256]{1,0:T(8,128)(2,1)S(1)}, u32[]{:S(2)}, u32[]{:S(2)}) collective-permute-start(bf16[512,256]{1,0:T(8,128)(2,1)S(1)} %pair.4), channel_id=1, source_target_pairs={{0,1},{1,2},{2,3},{3,0},{4,5},{5,6},{6,7},{7,4},{8,9},{9,10},{10,1... | collective-permute-start | bytes 786440 | tf_op jit(solution)/shard_map/ppermute | solution.py:426
  28.6 12.7 %collective-permute-start.3 = (bf16[512,256]{1,0:T(8,128)(2,1)S(1)}, bf16[512,256]{1,0:T(8,128)(2,1)S(1)}, u32[]{:S(2)}, u32[]{:S(2)}) collective-permute-start(bf16[512,256]{1,0:T(8,128)(2,1)S(1)} %pair.5), channel_id=1, source_target_pairs={{0,3},{1,0},{2,1},{3,2},{4,7},{5,4},{6,5},{7,6},{8,11},{9,8},{10,9... | collective-permute-start | bytes 786440 | tf_op jit(solution)/shard_map/ppermute | solution.py:427
  42.4 18.6 %copy-start.4 = (s32[512]{0:T(512)S(1)}, s32[512]{0:T(512)}, u32[]{:S(2)}) copy-start(s32[512]{0:T(512)} %param.13) | copy-start | bytes 6148
  42.4 41.4 %all-to-all-start = ((bf16[64,16,256]{2,1,0:T(8,128)(2,1)}), bf16[64,16,256]{2,1,0:T(8,128)(2,1)S(1)}, u32[]{:S(2)}, u32[]{:S(2)}) async-start(bf16[64,16,256]{2,1,0:T(8,128)(2,1)} %bitcast.2), calls=%async_computation | async-start | bytes 1048576 | tf_op jit(solution)/shard_map/all_to_all | solution.py:432
  58.3 14.5 %collective-permute-start.6 = (bf16[1024,256]{1,0:T(8,128)(2,1)}, bf16[1024,256]{1,0:T(8,128)(2,1)S(1)}, u32[]{:S(2)}, u32[]{:S(2)}) collective-permute-start(bf16[1024,256]{1,0:T(8,128)(2,1)} %get-tuple-element.52), channel_id=1, source_target_pairs={{0,1},{1,2},{2,3},{3,0},{4,5},{5,6},{6,7},{7,4},{8,9},{9,10},{10,1... | collective-permute-start | bytes 1572872 | tf_op jit(solution)/shard_map/ppermute | solution.py:467
  58.4 16.3 %collective-permute-start.8 = (bf16[1024,256]{1,0:T(8,128)(2,1)}, bf16[1024,256]{1,0:T(8,128)(2,1)S(1)}, u32[]{:S(2)}, u32[]{:S(2)}) collective-permute-start(bf16[1024,256]{1,0:T(8,128)(2,1)} %get-tuple-element.55), channel_id=1, source_target_pairs={{0,3},{1,0},{2,1},{3,2},{4,7},{5,4},{6,5},{7,6},{8,11},{9,8},{10,9... | collective-permute-start | bytes 1572872 | tf_op jit(solution)/shard_map/ppermute | solution.py:468
  72.8 0.8 copy-start.2
  74.6 9.2 %collective-permute-start.7 = (bf16[512,256]{1,0:T(8,128)(2,1)S(1)}, bf16[512,256]{1,0:T(8,128)(2,1)S(1)}, u32[]{:S(2)}, u32[]{:S(2)}) collective-permute-start(bf16[512,256]{1,0:T(8,128)(2,1)S(1)} %pair.6), channel_id=1, source_target_pairs={{0,1},{1,2},{2,3},{3,0},{4,5},{5,6},{6,7},{7,4},{8,9},{9,10},{10,1... | collective-permute-start | bytes 786440 | tf_op jit(solution)/shard_map/ppermute | solution.py:426
  74.7 0.8 copy-start.3
  76.5 7.3 %collective-permute-start.9 = (bf16[512,256]{1,0:T(8,128)(2,1)S(1)}, bf16[512,256]{1,0:T(8,128)(2,1)S(1)}, u32[]{:S(2)}, u32[]{:S(2)}) collective-permute-start(bf16[512,256]{1,0:T(8,128)(2,1)S(1)} %pair.7), channel_id=1, source_target_pairs={{0,3},{1,0},{2,1},{3,2},{4,7},{5,4},{6,5},{7,6},{8,11},{9,8},{10,9... | collective-permute-start | bytes 786440 | tf_op jit(solution)/shard_map/ppermute | solution.py:427
  83.8 34.7 %copy-start = (bf16[2048,512]{1,0:T(8,128)(2,1)S(1)}, bf16[2048,512]{1,0:T(8,128)(2,1)}, u32[]{:S(2)}) copy-start(bf16[2048,512]{1,0:T(8,128)(2,1)} %get-tuple-element.64.refs_5_) | copy-start | bytes 6291460
  83.8 34.7 %copy-start.1 = (bf16[2048,128]{1,0:T(8,128)(2,1)S(1)}, bf16[2048,128]{1,0:T(8,128)(2,1)}, u32[]{:S(2)}) copy-start(bf16[2048,128]{1,0:T(8,128)(2,1)} %get-tuple-element.65.refs_6_) | copy-start | bytes 1572868
  86.9 3.8 %collective-permute-start.11 = (f32[8,256]{1,0:T(8,128)S(1)}, f32[8,256]{1,0:T(8,128)S(1)}, u32[]{:S(2)}, u32[]{:S(2)}) collective-permute-start(f32[8,256]{1,0:T(8,128)S(1)} %get-tuple-element.66.mid_ref), channel_id=1, source_target_pairs={{0,3},{1,0},{2,1},{3,2},{4,7},{5,4},{6,5},{7,6},{8,11},{9,8},{10,9... | collective-permute-start | bytes 24584 | tf_op jit(solution)/shard_map/ppermute | solution.py:485
  89.9 3.7 %collective-permute-start.10 = (f32[8,256]{1,0:T(8,128)S(1)}, f32[8,256]{1,0:T(8,128)S(1)}, u32[]{:S(2)}, u32[]{:S(2)}) collective-permute-start(f32[8,256]{1,0:T(8,128)S(1)} %get-tuple-element.66.mid_ref), channel_id=1, source_target_pairs={{0,1},{1,2},{2,3},{3,0},{4,5},{5,6},{6,7},{7,4},{8,9},{9,10},{10,1... | collective-permute-start | bytes 24584 | tf_op jit(solution)/shard_map/ppermute | solution.py:484
  112.2 6.2 %collective-permute-start.12 = (bf16[32,8,256]{2,1,0:T(8,128)(2,1)S(1)}, bf16[32,8,256]{2,1,0:T(8,128)(2,1)S(1)}, u32[]{:S(2)}, u32[]{:S(2)}) collective-permute-start(bf16[32,8,256]{2,1,0:T(8,128)(2,1)S(1)} %all_to_all.25), channel_id=1, source_target_pairs={{0,4},{4,0},{1,5},{5,1},{2,6},{6,2},{3,7},{7,3},{8,12},{12,8},{9,1... | collective-permute-start | bytes 393224 | tf_op jit(solution)/shard_map/ppermute | solution.py:489
  121.4 2.5 %collective-permute-start.14 = (f32[8,256]{1,0:T(8,128)S(1)}, f32[8,256]{1,0:T(8,128)S(1)}, u32[]{:S(2)}, u32[]{:S(2)}) collective-permute-start(f32[8,256]{1,0:T(8,128)S(1)} %iterate.3.mid_ref), channel_id=1, source_target_pairs={{0,3},{1,0},{2,1},{3,2},{4,7},{5,4},{6,5},{7,6},{8,11},{9,8},{10,9... | collective-permute-start | bytes 24584 | tf_op jit(solution)/shard_map/ppermute | solution.py:485
  121.4 4.0 %collective-permute-start.13 = (f32[8,256]{1,0:T(8,128)S(1)}, f32[8,256]{1,0:T(8,128)S(1)}, u32[]{:S(2)}, u32[]{:S(2)}) collective-permute-start(f32[8,256]{1,0:T(8,128)S(1)} %iterate.3.mid_ref), channel_id=1, source_target_pairs={{0,1},{1,2},{2,3},{3,0},{4,5},{5,6},{6,7},{7,4},{8,9},{9,10},{10,1... | collective-permute-start | bytes 24584 | tf_op jit(solution)/shard_map/ppermute | solution.py:484
  138.0 3.9 %collective-permute-start.15 = (bf16[32,8,256]{2,1,0:T(8,128)(2,1)S(1)}, bf16[32,8,256]{2,1,0:T(8,128)(2,1)S(1)}, u32[]{:S(2)}, u32[]{:S(2)}) collective-permute-start(bf16[32,8,256]{2,1,0:T(8,128)(2,1)S(1)} %all_to_all.26), channel_id=1, source_target_pairs={{0,4},{4,0},{1,5},{5,1},{2,6},{6,2},{3,7},{7,3},{8,12},{12,8},{9,1... | collective-permute-start | bytes 393224 | tf_op jit(solution)/shard_map/ppermute | solution.py:489
  144.9 2.5 %collective-permute-start.17 = (f32[8,256]{1,0:T(8,128)S(1)}, f32[8,256]{1,0:T(8,128)S(1)}, u32[]{:S(2)}, u32[]{:S(2)}) collective-permute-start(f32[8,256]{1,0:T(8,128)S(1)} %iterate.4.mid_ref), channel_id=1, source_target_pairs={{0,3},{1,0},{2,1},{3,2},{4,7},{5,4},{6,5},{7,6},{8,11},{9,8},{10,9... | collective-permute-start | bytes 24584 | tf_op jit(solution)/shard_map/ppermute | solution.py:485
  144.9 3.8 %collective-permute-start.16 = (f32[8,256]{1,0:T(8,128)S(1)}, f32[8,256]{1,0:T(8,128)S(1)}, u32[]{:S(2)}, u32[]{:S(2)}) collective-permute-start(f32[8,256]{1,0:T(8,128)S(1)} %iterate.4.mid_ref), channel_id=1, source_target_pairs={{0,1},{1,2},{2,3},{3,0},{4,5},{5,6},{6,7},{7,4},{8,9},{9,10},{10,1... | collective-permute-start | bytes 24584 | tf_op jit(solution)/shard_map/ppermute | solution.py:484
  161.2 3.9 %collective-permute-start.18 = (bf16[32,8,256]{2,1,0:T(8,128)(2,1)S(1)}, bf16[32,8,256]{2,1,0:T(8,128)(2,1)S(1)}, u32[]{:S(2)}, u32[]{:S(2)}) collective-permute-start(bf16[32,8,256]{2,1,0:T(8,128)(2,1)S(1)} %all_to_all.27), channel_id=1, source_target_pairs={{0,4},{4,0},{1,5},{5,1},{2,6},{6,2},{3,7},{7,3},{8,12},{12,8},{9,1... | collective-permute-start | bytes 393224 | tf_op jit(solution)/shard_map/ppermute | solution.py:489
  168.1 2.5 %collective-permute-start.20 = (f32[8,256]{1,0:T(8,128)S(1)}, f32[8,256]{1,0:T(8,128)S(1)}, u32[]{:S(2)}, u32[]{:S(2)}) collective-permute-start(f32[8,256]{1,0:T(8,128)S(1)} %iterate.5.mid_ref), channel_id=1, source_target_pairs={{0,3},{1,0},{2,1},{3,2},{4,7},{5,4},{6,5},{7,6},{8,11},{9,8},{10,9... | collective-permute-start | bytes 24584 | tf_op jit(solution)/shard_map/ppermute | solution.py:485
  168.1 3.8 %collective-permute-start.19 = (f32[8,256]{1,0:T(8,128)S(1)}, f32[8,256]{1,0:T(8,128)S(1)}, u32[]{:S(2)}, u32[]{:S(2)}) collective-permute-start(f32[8,256]{1,0:T(8,128)S(1)} %iterate.5.mid_ref), channel_id=1, source_target_pairs={{0,1},{1,2},{2,3},{3,0},{4,5},{5,6},{6,7},{7,4},{8,9},{9,10},{10,1... | collective-permute-start | bytes 24584 | tf_op jit(solution)/shard_map/ppermute | solution.py:484
where the time goes:
time: 173 us
  starting transfers between devices  56.4 us (33%)
  blocking collectives  43.5 us (25%)
  Pallas kernels  38.5 us (22%)
  waiting for transfers between devices  32.1 us (19%)
  local copies, waits for them, and re-layouts  1.94 us (1%)
    all_to_all x3, blocking collectives, body(): lax.all_to_all(block, ('y', 'z'), split_axis=0, concat_axis=0, tiled=True)  43.5 us
    all_to_all x2, starting transfers between devices, exchange(): return lax.all_to_all(value, BL, split_axis=0, concat_axis=0, tiled=True)  25.4 us
    pallas_call x4, Pallas kernels, iterate(): pl.pallas_call(iterate_kernel(first), out_shape=[jax.ShapeDtypeStruct((8,...  11.9 us
    ppermute x3, starting transfers between devices, body(): others = lax.ppermute(everyone, 'core', [(0, 1), (1, 0)])  11.1 us
    ppermute x1, waiting for transfers between devices, body(): from_low = lax.ppermute(going_up, 'ch', UP)  8.07 us
    pallas_call x2, Pallas kernels, degrid(): pl.pallas_call(degrid_kernel(count), out_shape=[half] * (2 * count) + [ta...  7.21 us
    pallas_call x2, Pallas kernels, late_degrid(): pl.pallas_call(late_kernel(jobs), out_shape=shapes, in_specs=[vmem, anywh...  7.02 us
    ppermute x4, waiting for transfers between devices, body(): low = lax.ppermute(mid, 'ch', UP)  6.96 us
  transfers between devices with their start and end apart: 23, of which 16 were waited for; matrix products, arithmetic and copies ran while one was open for 0% of the time, Pallas kernels for 13%

commit v1 on v0

--- a/solution.py
+++ b/solution.py
@@ -82,12 +82,16 @@
     )(where, tile_of, in_hbm(kernel), *([in_hbm(facet_grid)] * count))
 
 
-def late_kernel(jobs):
+def late_kernel(jobs, extra):
     def run(pay_ref, first_ref, second_ref, third_ref, *refs):
-        outs, (lhs_ref, table_ref, sems) = refs[:-3], refs[-3:]
+        arrived, outs, (lhs_ref, table_ref, add_ref, sems) = refs[:extra], refs[extra:-4], refs[-4:]
         loads = [
             pltpu.make_async_copy(source, table_ref.at[index], sems.at[index])
             for index, source in enumerate((first_ref, second_ref, third_ref))
+        ]
+        loads += [
+            pltpu.make_async_copy(source.at[:HALF], add_ref.at[index], sems.at[3 + index])
+            for index, source in enumerate(arrived)
         ]
         for load in loads:
             load.start()
@@ -111,27 +115,31 @@
         for half in range(2):
             for index, out, start in jobs[half]:
                 source = lhs_ref[half * HALF : (half + 1) * HALF, :]
-                outs[out][start : start + HALF, :] = nt(source, table_ref[index]).astype(BF16)
+                value = nt(source, table_ref[index])
+                if out < extra:
+                    value = value + add_ref[out].astype(F32)
+                outs[out][start : start + HALF, :] = value.astype(BF16)
 
     return run
 
 
-def late_degrid(payload, tables, jobs, shapes):
+def late_degrid(payload, tables, jobs, shapes, arrived=()):
     vmem = pl.BlockSpec(memory_space=pltpu.VMEM)
     anywhere = pl.BlockSpec(memory_space=pl.ANY)
     return pl.pallas_call(
-        late_kernel(jobs),
+        late_kernel(jobs, len(arrived)),
         out_shape=shapes,
-        in_specs=[vmem, anywhere, anywhere, anywhere],
+        in_specs=[vmem] + [anywhere] * (3 + len(arrived)),
         out_specs=[vmem] * len(shapes),
         scratch_shapes=[
             pltpu.VMEM((1024, 1024), BF16),
             pltpu.VMEM((3, 256, 1024), BF16),
-            pltpu.SemaphoreType.DMA((3,)),
+            pltpu.VMEM((2, HALF, 256), BF16),
+            pltpu.SemaphoreType.DMA((5,)),
         ],
         compiler_params=SMALL,
         name="late",
-    )(payload, *[in_hbm(table) for table in tables])
+    )(payload, *[in_hbm(item) for item in (*tables, *arrived)])
 
 
 def payload_kernel(tile_ref, obs_ref, flag_ref, pair_ref, kern_ref, out_ref, kept_ref, stacked_ref, sem):
@@ -466,11 +474,16 @@
     )
     from_low = lax.ppermute(going_up, "ch", UP)
     from_high = lax.ppermute(going_down, "ch", DOWN)
-    next_a, prev_b, own_a, own_b = late_degrid(
-        arrived, (table1, table3, table0), (((0, 0, 0), (2, 2, 0)), ((1, 1, 0), (2, 3, 0))), [half, half, away, away]
+    sum_a, sum_b, own_a, own_b = late_degrid(
+        arrived,
+        (table1, table3, table0),
+        (((0, 0, 0), (2, 2, 0)), ((1, 1, 0), (2, 3, 0))),
+        [half, half, away, away],
+        (from_low, from_high),
     )
     ohq, ohp, opt, vis_re, vis_im, kept_b = make_setup(arrived, order_row, own_row)
-    chain_a, chain_b, *_ = last_legs(from_low, from_high, None, None, next_a, prev_b)
+    chain_a = lax.ppermute(sum_a, "ch", UP)
+    chain_b = lax.ppermute(sum_b, "ch", DOWN)
     model_a = exchange(model_a.reshape(64, 16, 256)).reshape(1024, 256)
 
     for step in range(ITERS):

time: 173 us -> 174 us (level)
  waiting for transfers between devices: 32.1 us -> 36.1 us
  Pallas kernels: 38.5 us -> 36.6 us
    ppermute x1, waiting for transfers between devices: 8.07 us -> 11.4 us  [body(): from_low = lax.ppermute(going_up, 'ch', UP)]
    ppermute x0 -> x2, starting transfers between devices: none -> 2.75 us  [the longest x1 2.66 us: body(): chain_b = lax.ppermute(sum_b, 'ch', DOWN)]
    ppermute x2 -> x1, starting transfers between devices: 5.47 us -> 2.73 us  [last_legs(): chain_b = lax.ppermute(pair_sum(chain_b, prev_b), 'ch', DOWN)]
    pallas_call x4 -> x2, Pallas kernels: 2.16 us -> 0.14 us  [pair_sum(): pl.pallas_call(pair_kernel, out_shape=jax.ShapeDtypeStruct((HALF, 256), B...]
    ppermute x2 -> x1, waiting for transfers between devices: 5.62 us -> 5.62 us  [last_legs(): chain_a = lax.ppermute(pair_sum(chain_a, next_a), 'ch', UP)]
  transfers between devices with their start and end apart: 23 -> 23, of which waited for: 16 -> 17; matrix products, arithmetic and copies ran while one was open for 0% -> 0% of each run, Pallas kernels for 13% -> 11%
where the time goes in v1:
time: 174 us
  starting transfers between devices  55.9 us (32%)
  blocking collectives  43.5 us (25%)
  Pallas kernels  36.6 us (21%)
  waiting for transfers between devices  36.1 us (21%)
    all_to_all x3, blocking collectives, body(): lax.all_to_all(block, ('y', 'z'), split_axis=0, concat_axis=0, tiled=True)  43.5 us
    all_to_all x2, starting transfers between devices, exchange(): return lax.all_to_all(value, BL, split_axis=0, concat_axis=0, tiled=True)  25.4 us
    pallas_call x4, Pallas kernels, iterate(): pl.pallas_call(iterate_kernel(first), out_shape=[jax.ShapeDtypeStruct((8,...  11.8 us
    ppermute x1, waiting for transfers between devices, body(): from_low = lax.ppermute(going_up, 'ch', UP)  11.4 us
    ppermute x3, starting transfers between devices, body(): others = lax.ppermute(everyone, 'core', [(0, 1), (1, 0)])  11.1 us
    pallas_call x2, Pallas kernels, degrid(): pl.pallas_call(degrid_kernel(count), out_shape=[half] * (2 * count) + [ta...  7.21 us
    pallas_call x2, Pallas kernels, late_degrid(): pl.pallas_call(late_kernel(jobs, len(arrived)), out_shape=shapes, in_spec...  7.2 us
    ppermute x4, waiting for transfers between devices, body(): low = lax.ppermute(mid, 'ch', UP)  6.96 us
  transfers between devices with their start and end apart: 23, of which 17 were waited for; matrix products, arithmetic and copies ran while one was open for 0% of the time, Pallas kernels for 11%

profile of v1, /device:TPU:1, one launch (start us, length us, event | category | flops | bytes accessed | tf_op | source)
XLA Modules:
  0.0 173.7 jit_solution(8842339889491318160)
XLA Ops:
  0.0 3.6 %payload.1 = (bf16[64,24,256]{2,1,0:T(8,128)(2,1)}, bf16[1024,128]{1,0:T(8,128)(2,1)S(1)}) custom-call(s32[4]{0:T(128)} %tile_ref.5, bf16[16,2,2048]{2,1,0:T(2,128)(2,1)} %obs_ref.1, s32[16,2048]{1,0:T(8,128)} %flag_ref.1, s32[2,2048]{1,0:T(2,128)} %pair_ref.1, bf16[64,32,256]{2,1,0:T(8,128)(2,1)} %bitcast.33), custom_call_target="tpu_custom_call" | custom-call | tf_op jit(solution)/shard_map/payload/pallas_call | solution.py:182
  3.6 13.2 %all-to-all-start.1 = ((bf16[64,24,256]{2,1,0:T(8,128)(2,1)}), bf16[64,24,256]{2,1,0:T(8,128)(2,1)S(1)}, u32[]{:S(2)}, u32[]{:S(2)}) async-start(bf16[64,24,256]{2,1,0:T(8,128)(2,1)} %get-tuple-element.48), calls=%async_computation.1 | async-start | bytes 1572864 | tf_op jit(solution)/shard_map/all_to_all | solution.py:440
  16.7 3.0 %shard_map.74 = (bf16[512,256]{1,0:T(8,128)(2,1)S(1)}, bf16[512,256]{1,0:T(8,128)(2,1)S(1)}, bf16[256,1024]{1,0:T(8,128)(2,1)}) custom-call(s32[1]{0:T(128)} %bitcast.where_ref, s32[4]{0:T(128)} %tile_ref.5, bf16[64,32,256]{2,1,0:T(8,128)(2,1)} %bitcast.34, bf16[4,64,16,256]{3,2,1,0:T(8,128)(2,1)} %refs_0_.3), custom_call_target="tpu_custom_call" | custom-call | tf_op jit(solution)/shard_map/pallas_call | solution.py:72
  19.7 1.2 collective-permute-start
  21.0 1.5 collective-permute-start.2
  22.4 4.2 %shard_map.73 = (bf16[512,256]{1,0:T(8,128)(2,1)S(1)}, bf16[512,256]{1,0:T(8,128)(2,1)S(1)}, bf16[512,256]{1,0:T(8,128)(2,1)S(1)}, bf16[512,256]{1,0:T(8,128)(2,...) custom-call(s32[1]{0:T(128)} %bitcast.where_ref, ...), custom_call_target="tpu_custom_call" | custom-call | tf_op jit(solution)/shard_map/pallas_call | solution.py:72
  26.6 1.3 collective-permute-start.4
  28.1 0.3 collective-permute-done.left_ref
  28.6 2.7 %collective-permute-start.3 = (bf16[512,256]{1,0:T(8,128)(2,1)S(1)}, bf16[512,256]{1,0:T(8,128)(2,1)S(1)}, u32[]{:S(2)}, u32[]{:S(2)}) collective-permute-start(bf16[512,256]{1,0:T(8,128)(2,1)S(1)} %pair.3), channel_id=1, source_target_pairs={{0,3},{1,0},{2,1},{3,2},{4,7},{5,4},{6,5},{7,6},{8,11},{9,8},{10,9... | collective-permute-start | bytes 786440 | tf_op jit(solution)/shard_map/ppermute | solution.py:435
  31.3 2.1 %collective-permute-done.4.near_a = bf16[512,256]{1,0:T(8,128)(2,1)S(1)} collective-permute-done((bf16[512,256]{1,0:T(8,128)(2,1)S(1)}, bf16[512,256]{1,0:T(8,128)(2,1)S(1)}, u32[]{:S(2)}, u32[]{:S(2)}) %collective-permute-start.4) | collective-permute-done | bytes 262176 | tf_op jit(solution)/shard_map/ppermute | solution.py:461
  33.5 2.2 %collective-permute-done.5.near_b = bf16[512,256]{1,0:T(8,128)(2,1)S(1)} collective-permute-done((bf16[512,256]{1,0:T(8,128)(2,1)S(1)}, bf16[512,256]{1,0:T(8,128)(2,1)S(1)}, u32[]{:S(2)}, u32[]{:S(2)}) %collective-permute-start.5) | collective-permute-done | bytes 262176 | tf_op jit(solution)/shard_map/ppermute | solution.py:462
  35.7 5.6 %collective-permute-done.1.chain_a = bf16[512,256]{1,0:T(8,128)(2,1)S(1)} collective-permute-done((bf16[512,256]{1,0:T(8,128)(2,1)S(1)}, bf16[512,256]{1,0:T(8,128)(2,1)S(1)}, u32[]{:S(2)}, u32[]{:S(2)}) %collective-permute-start.1) | collective-permute-done | bytes 262176 | tf_op jit(solution)/shard_map/ppermute | solution.py:434
  41.3 1.1 add.19
  42.4 12.2 %all-to-all-start = ((bf16[64,16,256]{2,1,0:T(8,128)(2,1)}), bf16[64,16,256]{2,1,0:T(8,128)(2,1)S(1)}, u32[]{:S(2)}, u32[]{:S(2)}) async-start(bf16[64,16,256]{2,1,0:T(8,128)(2,1)} %bitcast.2), calls=%async_computation | async-start | bytes 1048576 | tf_op jit(solution)/shard_map/all_to_all | solution.py:440
  54.6 3.7 %late.2 = (bf16[1024,256]{1,0:T(8,128)(2,1)}, bf16[1024,256]{1,0:T(8,128)(2,1)}) custom-call(bf16[64,24,256]{2,1,0:T(8,128)(2,1)S(1)} %all-to-all-done.1.pay_ref, bf16[256,1024]{1,0:T(8,128)(2,1)} %get-tuple-element.52.first_ref, bf16[256,1024]{1,0:T(8,128)(2,1)} %get-tuple-element.50.second_ref, bf16[256,1024]{1,0:T(8,128)(2,1)} %get-tuple-element.49.third_ref.first_ref), custom_call_target="tpu_custom_call" | custom-call | tf_op jit(solution)/shard_map/late/pallas_call | solution.py:129
  58.4 2.7 %collective-permute-start.7 = (bf16[1024,256]{1,0:T(8,128)(2,1)}, bf16[1024,256]{1,0:T(8,128)(2,1)S(1)}, u32[]{:S(2)}, u32[]{:S(2)}) collective-permute-start(bf16[1024,256]{1,0:T(8,128)(2,1)} %get-tuple-element.54), channel_id=1, source_target_pairs={{0,3},{1,0},{2,1},{3,2},{4,7},{5,4},{6,5},{7,6},{8,11},{9,8},{10,9... | collective-permute-start | bytes 1572872 | tf_op jit(solution)/shard_map/ppermute | solution.py:476
  61.4 11.4 %collective-permute-done.6.refs_0_.refs_9_ = bf16[1024,256]{1,0:T(8,128)(2,1)S(1)} collective-permute-done((bf16[1024,256]{1,0:T(8,128)(2,1)}, bf16[1024,256]{1,0:T(8,128)(2,1)S(1)}, u32[]{:S(2)}, u32[]{:S(2)}) %collective-permute-start.6) | collective-permute-done | bytes 524320 | tf_op jit(solution)/shard_map/ppermute | solution.py:475
  72.8 0.8 copy-done.2
  73.8 3.5 %late.3 = (bf16[512,256]{1,0:T(8,128)(2,1)S(1)}, bf16[512,256]{1,0:T(8,128)(2,1)S(1)}, bf16[512,256]{1,0:T(8,128)(2,1)}, bf16[512,256]{1,0:T(8,128)(2,1)}) custom-call(bf16[64,24,256]{2,1,0:T(8,128)(2,1)S(1)} %all-to-all-done.1.pay_ref, bf16[256,1024]{1,0:T(8,128)(2,1)} %get-tuple-element.49.third_ref.first_ref, ...), custom_call_target="tpu_custom_call" | custom-call | tf_op jit(solution)/shard_map/late/pallas_call | solution.py:129
  77.4 2.7 %collective-permute-start.9 = (bf16[512,256]{1,0:T(8,128)(2,1)S(1)}, bf16[512,256]{1,0:T(8,128)(2,1)S(1)}, u32[]{:S(2)}, u32[]{:S(2)}) collective-permute-start(bf16[512,256]{1,0:T(8,128)(2,1)S(1)} %get-tuple-element.56), channel_id=1, source_target_pairs={{0,3},{1,0},{2,1},{3,2},{4,7},{5,4},{6,5},{7,6},{8,11},{9,8},{10,9... | collective-permute-start | bytes 786440 | tf_op jit(solution)/shard_map/ppermute | solution.py:486
  80.3 4.3 %setup.1 = (bf16[2048,512]{1,0:T(8,128)(2,1)}, bf16[2048,128]{1,0:T(8,128)(2,1)}, bf16[16,2048]{1,0:T(8,128)(2,1)S(1)}, bf16[2048,128]{1,0:T(8,128)(2,1)S(1)}, b...) custom-call(bf16[64,24,256]{2,1,0:T(8,128)(2,1)S(1)} %all-to-all-done.1.pay_ref, f32[1,512]{1,0:T(1,128)S(1)} %bitcast.32, ...), custom_call_target="tpu_custom_call" | custom-call | tf_op jit(solution)/shard_map/setup/pallas_call | solution.py:247
  84.6 0.6 collective-permute-done.8.refs_1_
  85.2 3.1 %iterate0.1 = (f32[8,256]{1,0:T(8,128)S(1)}, bf16[1024,256]{1,0:T(8,128)(2,1)S(1)}) custom-call(bf16[1024,256]{1,0:T(8,128)(2,1)S(1)} %bitcast.22, bf16[512,256]{1,0:T(8,128)(2,1)S(1)} %collective-permute-done.8.refs_1_, bf16[512,256]{1,0:T(8,128)(2,1)S(1)} %collective-permute-done.9.refs_2_, bf16[16,2048]{1,0:T(8,128)(2,1)S(1)} %get-tuple-element.57.refs_3_.refs_2_, ...), custom_call_target="tpu_custom_call" | custom-call | tf_op jit(solution)/shard_map/iterate0/pallas_call | solution.py:336
  88.3 2.5 %collective-permute-start.11 = (f32[8,256]{1,0:T(8,128)S(1)}, f32[8,256]{1,0:T(8,128)S(1)}, u32[]{:S(2)}, u32[]{:S(2)}) collective-permute-start(f32[8,256]{1,0:T(8,128)S(1)} %get-tuple-element.66.mid_ref), channel_id=1, source_target_pairs={{0,3},{1,0},{2,1},{3,2},{4,7},{5,4},{6,5},{7,6},{8,11},{9,8},{10,9... | collective-permute-start | bytes 24584 | tf_op jit(solution)/shard_map/ppermute | solution.py:498
  90.7 0.8 collective-permute-done.11.high_ref
  91.5 2.9 %collective-permute-done.10.low_ref = f32[8,256]{1,0:T(8,128)S(1)} collective-permute-done((f32[8,256]{1,0:T(8,128)S(1)}, f32[8,256]{1,0:T(8,128)S(1)}, u32[]{:S(2)}, u32[]{:S(2)}) %collective-permute-start.10) | collective-permute-done | bytes 8224 | tf_op jit(solution)/shard_map/ppermute | solution.py:497
  94.5 18.6 %all_to_all.25 = bf16[32,8,256]{2,1,0:T(8,128)(2,1)S(1)} all-to-all(bf16[32,8,256]{2,1,0:T(8,128)(2,1)S(1)} %get-tuple-element.67), channel_id=1, replica_groups=mesh['y'=4,'z'=8,'core'=2,'ch'=4] {'y','z'}, dimensions={0} | all-to-all | bytes 262144 | tf_op jit(solution)/shard_map/all_to_all | solution.py:501
  113.1 5.2 %collective-permute-start.12 = (bf16[32,8,256]{2,1,0:T(8,128)(2,1)S(1)}, bf16[32,8,256]{2,1,0:T(8,128)(2,1)S(1)}, u32[]{:S(2)}, u32[]{:S(2)}) collective-permute-start(bf16[32,8,256]{2,1,0:T(8,128)(2,1)S(1)} %all_to_all.25), channel_id=1, source_target_pairs={{0,4},{4,0},{1,5},{5,1},{2,6},{6,2},{3,7},{7,3},{8,12},{12,8},{9,1... | collective-permute-start | bytes 393224 | tf_op jit(solution)/shard_map/ppermute | solution.py:502
  118.4 1.0 collective-permute-done.12
  119.4 2.9 %iterate.3.mid_ref = f32[8,256]{1,0:T(8,128)S(1)} custom-call(bf16[1024,256]{1,0:T(8,128)(2,1)S(1)} %bitcast.23, bf16[1024,256]{1,0:T(8,128)(2,1)S(1)} %get-tuple-element.63.refs_1_, bf16[16,2048]{1,0:T(8,128)(2,1)S(1)} %get-tuple-element.57.refs_3_.refs_2_, bf16[2048,128]{1,0:T(8,128)(2,1)S(1)} %get-tuple-element.58.refs_4_.refs_3_, ...), custom_call_target="tpu_custom_call" | custom-call | tf_op jit(solution)/shard_map/iterate/pallas_call | solution.py:336
  122.3 1.5 collective-permute-start.13
  123.8 1.0 collective-permute-done.14.high_ref
  124.8 1.5 collective-permute-done.13.low_ref
  126.4 12.5 %all_to_all.26 = bf16[32,8,256]{2,1,0:T(8,128)(2,1)S(1)} all-to-all(bf16[32,8,256]{2,1,0:T(8,128)(2,1)S(1)} %get-tuple-element.69), channel_id=1, replica_groups=mesh['y'=4,'z'=8,'core'=2,'ch'=4] {'y','z'}, dimensions={0} | all-to-all | bytes 262144 | tf_op jit(solution)/shard_map/all_to_all | solution.py:501
  138.9 2.9 %collective-permute-start.15 = (bf16[32,8,256]{2,1,0:T(8,128)(2,1)S(1)}, bf16[32,8,256]{2,1,0:T(8,128)(2,1)S(1)}, u32[]{:S(2)}, u32[]{:S(2)}) collective-permute-start(bf16[32,8,256]{2,1,0:T(8,128)(2,1)S(1)} %all_to_all.26), channel_id=1, source_target_pairs={{0,4},{4,0},{1,5},{5,1},{2,6},{6,2},{3,7},{7,3},{8,12},{12,8},{9,1... | collective-permute-start | bytes 393224 | tf_op jit(solution)/shard_map/ppermute | solution.py:502
  141.9 1.0 collective-permute-done.15
  142.8 2.9 %iterate.4.mid_ref = f32[8,256]{1,0:T(8,128)S(1)} custom-call(bf16[1024,256]{1,0:T(8,128)(2,1)S(1)} %bitcast.24, bf16[1024,256]{1,0:T(8,128)(2,1)S(1)} %get-tuple-element.63.refs_1_, bf16[16,2048]{1,0:T(8,128)(2,1)S(1)} %get-tuple-element.57.refs_3_.refs_2_, bf16[2048,128]{1,0:T(8,128)(2,1)S(1)} %get-tuple-element.58.refs_4_.refs_3_, ...), custom_call_target="tpu_custom_call" | custom-call | tf_op jit(solution)/shard_map/iterate/pallas_call | solution.py:336
  145.8 1.5 collective-permute-start.16
  147.3 1.0 collective-permute-done.17.high_ref
  148.3 1.3 collective-permute-done.16.low_ref
  149.7 12.4 %all_to_all.27 = bf16[32,8,256]{2,1,0:T(8,128)(2,1)S(1)} all-to-all(bf16[32,8,256]{2,1,0:T(8,128)(2,1)S(1)} %get-tuple-element.71), channel_id=1, replica_groups=mesh['y'=4,'z'=8,'core'=2,'ch'=4] {'y','z'}, dimensions={0} | all-to-all | bytes 262144 | tf_op jit(solution)/shard_map/all_to_all | solution.py:501
  162.1 2.9 %collective-permute-start.18 = (bf16[32,8,256]{2,1,0:T(8,128)(2,1)S(1)}, bf16[32,8,256]{2,1,0:T(8,128)(2,1)S(1)}, u32[]{:S(2)}, u32[]{:S(2)}) collective-permute-start(bf16[32,8,256]{2,1,0:T(8,128)(2,1)S(1)} %all_to_all.27), channel_id=1, source_target_pairs={{0,4},{4,0},{1,5},{5,1},{2,6},{6,2},{3,7},{7,3},{8,12},{12,8},{9,1... | collective-permute-start | bytes 393224 | tf_op jit(solution)/shard_map/ppermute | solution.py:502
  165.0 1.0 collective-permute-done.18
  166.0 2.9 %iterate.5.mid_ref = f32[8,256]{1,0:T(8,128)S(1)} custom-call(bf16[1024,256]{1,0:T(8,128)(2,1)S(1)} %bitcast.25, bf16[1024,256]{1,0:T(8,128)(2,1)S(1)} %get-tuple-element.63.refs_1_, bf16[16,2048]{1,0:T(8,128)(2,1)S(1)} %get-tuple-element.57.refs_3_.refs_2_, bf16[2048,128]{1,0:T(8,128)(2,1)S(1)} %get-tuple-element.58.refs_4_.refs_3_, ...), custom_call_target="tpu_custom_call" | custom-call | tf_op jit(solution)/shard_map/iterate/pallas_call | solution.py:336
  168.9 1.5 collective-permute-start.19
  170.4 1.0 collective-permute-done.20.high_ref
  171.5 1.3 collective-permute-done.19.low_ref
  172.7 1.0 finish.1
  (38 shorter events, 1.5 us)
Async XLA Ops:
  3.6 38.8 %all-to-all-start.1 = ((bf16[64,24,256]{2,1,0:T(8,128)(2,1)}), bf16[64,24,256]{2,1,0:T(8,128)(2,1)S(1)}, u32[]{:S(2)}, u32[]{:S(2)}) async-start(bf16[64,24,256]{2,1,0:T(8,128)(2,1)} %get-tuple-element.48), calls=%async_computation.1 | async-start | bytes 1572864 | tf_op jit(solution)/shard_map/all_to_all | solution.py:440
  19.7 8.6 %collective-permute-start = (bf16[512,256]{1,0:T(8,128)(2,1)S(1)}, bf16[512,256]{1,0:T(8,128)(2,1)S(1)}, u32[]{:S(2)}, u32[]{:S(2)}) collective-permute-start(bf16[512,256]{1,0:T(8,128)(2,1)S(1)} %get-tuple-element.41), channel_id=1, source_target_pairs={{0,1},{1,2},{2,3},{3,0},{4,5},{5,6},{6,7},{7,4},{8,9},{9,10},{10,1... | collective-permute-start | bytes 786440 | tf_op jit(solution)/shard_map/ppermute | solution.py:456
  21.0 7.6 %collective-permute-start.2 = (bf16[512,256]{1,0:T(8,128)(2,1)S(1)}, bf16[512,256]{1,0:T(8,128)(2,1)S(1)}, u32[]{:S(2)}, u32[]{:S(2)}) collective-permute-start(bf16[512,256]{1,0:T(8,128)(2,1)S(1)} %get-tuple-element.43), channel_id=1, source_target_pairs={{0,3},{1,0},{2,1},{3,2},{4,7},{5,4},{6,5},{7,6},{8,11},{9,8},{10,9... | collective-permute-start | bytes 786440 | tf_op jit(solution)/shard_map/ppermute | solution.py:457
  26.6 6.9 %collective-permute-start.4 = (bf16[512,256]{1,0:T(8,128)(2,1)S(1)}, bf16[512,256]{1,0:T(8,128)(2,1)S(1)}, u32[]{:S(2)}, u32[]{:S(2)}) collective-permute-start(bf16[512,256]{1,0:T(8,128)(2,1)S(1)} %get-tuple-element.45), channel_id=1, source_target_pairs={{0,3},{1,0},{2,1},{3,2},{4,7},{5,4},{6,5},{7,6},{8,11},{9,8},{10,9... | collective-permute-start | bytes 786440 | tf_op jit(solution)/shard_map/ppermute | solution.py:461
  27.9 7.8 %collective-permute-start.5 = (bf16[512,256]{1,0:T(8,128)(2,1)S(1)}, bf16[512,256]{1,0:T(8,128)(2,1)S(1)}, u32[]{:S(2)}, u32[]{:S(2)}) collective-permute-start(bf16[512,256]{1,0:T(8,128)(2,1)S(1)} %get-tuple-element.46), channel_id=1, source_target_pairs={{0,1},{1,2},{2,3},{3,0},{4,5},{5,6},{6,7},{7,4},{8,9},{9,10},{10,1... | collective-permute-start | bytes 786440 | tf_op jit(solution)/shard_map/ppermute | solution.py:462
  28.4 12.9 %collective-permute-start.1 = (bf16[512,256]{1,0:T(8,128)(2,1)S(1)}, bf16[512,256]{1,0:T(8,128)(2,1)S(1)}, u32[]{:S(2)}, u32[]{:S(2)}) collective-permute-start(bf16[512,256]{1,0:T(8,128)(2,1)S(1)} %pair.2), channel_id=1, source_target_pairs={{0,1},{1,2},{2,3},{3,0},{4,5},{5,6},{6,7},{7,4},{8,9},{9,10},{10,1... | collective-permute-start | bytes 786440 | tf_op jit(solution)/shard_map/ppermute | solution.py:434
  28.6 12.7 %collective-permute-start.3 = (bf16[512,256]{1,0:T(8,128)(2,1)S(1)}, bf16[512,256]{1,0:T(8,128)(2,1)S(1)}, u32[]{:S(2)}, u32[]{:S(2)}) collective-permute-start(bf16[512,256]{1,0:T(8,128)(2,1)S(1)} %pair.3), channel_id=1, source_target_pairs={{0,3},{1,0},{2,1},{3,2},{4,7},{5,4},{6,5},{7,6},{8,11},{9,8},{10,9... | collective-permute-start | bytes 786440 | tf_op jit(solution)/shard_map/ppermute | solution.py:435
  42.4 18.7 %copy-start.4 = (s32[512]{0:T(512)S(1)}, s32[512]{0:T(512)}, u32[]{:S(2)}) copy-start(s32[512]{0:T(512)} %param.13) | copy-start | bytes 6148
  42.4 42.2 %all-to-all-start = ((bf16[64,16,256]{2,1,0:T(8,128)(2,1)}), bf16[64,16,256]{2,1,0:T(8,128)(2,1)S(1)}, u32[]{:S(2)}, u32[]{:S(2)}) async-start(bf16[64,16,256]{2,1,0:T(8,128)(2,1)} %bitcast.2), calls=%async_computation | async-start | bytes 1048576 | tf_op jit(solution)/shard_map/all_to_all | solution.py:440
  58.3 14.5 %collective-permute-start.6 = (bf16[1024,256]{1,0:T(8,128)(2,1)}, bf16[1024,256]{1,0:T(8,128)(2,1)S(1)}, u32[]{:S(2)}, u32[]{:S(2)}) collective-permute-start(bf16[1024,256]{1,0:T(8,128)(2,1)} %get-tuple-element.53), channel_id=1, source_target_pairs={{0,1},{1,2},{2,3},{3,0},{4,5},{5,6},{6,7},{7,4},{8,9},{9,10},{10,1... | collective-permute-start | bytes 1572872 | tf_op jit(solution)/shard_map/ppermute | solution.py:475
  58.4 14.4 %collective-permute-start.7 = (bf16[1024,256]{1,0:T(8,128)(2,1)}, bf16[1024,256]{1,0:T(8,128)(2,1)S(1)}, u32[]{:S(2)}, u32[]{:S(2)}) collective-permute-start(bf16[1024,256]{1,0:T(8,128)(2,1)} %get-tuple-element.54), channel_id=1, source_target_pairs={{0,3},{1,0},{2,1},{3,2},{4,7},{5,4},{6,5},{7,6},{8,11},{9,8},{10,9... | collective-permute-start | bytes 1572872 | tf_op jit(solution)/shard_map/ppermute | solution.py:476
  72.8 0.8 copy-start.2
  72.8 1.0 copy-start.3
  77.3 7.8 %collective-permute-start.8 = (bf16[512,256]{1,0:T(8,128)(2,1)S(1)}, bf16[512,256]{1,0:T(8,128)(2,1)S(1)}, u32[]{:S(2)}, u32[]{:S(2)}) collective-permute-start(bf16[512,256]{1,0:T(8,128)(2,1)S(1)} %get-tuple-element.55), channel_id=1, source_target_pairs={{0,1},{1,2},{2,3},{3,0},{4,5},{5,6},{6,7},{7,4},{8,9},{9,10},{10,1... | collective-permute-start | bytes 786440 | tf_op jit(solution)/shard_map/ppermute | solution.py:485
  77.4 7.7 %collective-permute-start.9 = (bf16[512,256]{1,0:T(8,128)(2,1)S(1)}, bf16[512,256]{1,0:T(8,128)(2,1)S(1)}, u32[]{:S(2)}, u32[]{:S(2)}) collective-permute-start(bf16[512,256]{1,0:T(8,128)(2,1)S(1)} %get-tuple-element.56), channel_id=1, source_target_pairs={{0,3},{1,0},{2,1},{3,2},{4,7},{5,4},{6,5},{7,6},{8,11},{9,8},{10,9... | collective-permute-start | bytes 786440 | tf_op jit(solution)/shard_map/ppermute | solution.py:486
  85.2 34.2 %copy-start = (bf16[2048,512]{1,0:T(8,128)(2,1)S(1)}, bf16[2048,512]{1,0:T(8,128)(2,1)}, u32[]{:S(2)}) copy-start(bf16[2048,512]{1,0:T(8,128)(2,1)} %get-tuple-element.64.refs_5_) | copy-start | bytes 6291460
  85.2 34.2 %copy-start.1 = (bf16[2048,128]{1,0:T(8,128)(2,1)S(1)}, bf16[2048,128]{1,0:T(8,128)(2,1)}, u32[]{:S(2)}) copy-start(bf16[2048,128]{1,0:T(8,128)(2,1)} %get-tuple-element.65.refs_6_) | copy-start | bytes 1572868
  88.3 3.3 %collective-permute-start.11 = (f32[8,256]{1,0:T(8,128)S(1)}, f32[8,256]{1,0:T(8,128)S(1)}, u32[]{:S(2)}, u32[]{:S(2)}) collective-permute-start(f32[8,256]{1,0:T(8,128)S(1)} %get-tuple-element.66.mid_ref), channel_id=1, source_target_pairs={{0,3},{1,0},{2,1},{3,2},{4,7},{5,4},{6,5},{7,6},{8,11},{9,8},{10,9... | collective-permute-start | bytes 24584 | tf_op jit(solution)/shard_map/ppermute | solution.py:498
  90.7 3.7 %collective-permute-start.10 = (f32[8,256]{1,0:T(8,128)S(1)}, f32[8,256]{1,0:T(8,128)S(1)}, u32[]{:S(2)}, u32[]{:S(2)}) collective-permute-start(f32[8,256]{1,0:T(8,128)S(1)} %get-tuple-element.66.mid_ref), channel_id=1, source_target_pairs={{0,1},{1,2},{2,3},{3,0},{4,5},{5,6},{6,7},{7,4},{8,9},{9,10},{10,1... | collective-permute-start | bytes 24584 | tf_op jit(solution)/shard_map/ppermute | solution.py:497
  113.1 6.2 %collective-permute-start.12 = (bf16[32,8,256]{2,1,0:T(8,128)(2,1)S(1)}, bf16[32,8,256]{2,1,0:T(8,128)(2,1)S(1)}, u32[]{:S(2)}, u32[]{:S(2)}) collective-permute-start(bf16[32,8,256]{2,1,0:T(8,128)(2,1)S(1)} %all_to_all.25), channel_id=1, source_target_pairs={{0,4},{4,0},{1,5},{5,1},{2,6},{6,2},{3,7},{7,3},{8,12},{12,8},{9,1... | collective-permute-start | bytes 393224 | tf_op jit(solution)/shard_map/ppermute | solution.py:502
  122.3 2.5 %collective-permute-start.14 = (f32[8,256]{1,0:T(8,128)S(1)}, f32[8,256]{1,0:T(8,128)S(1)}, u32[]{:S(2)}, u32[]{:S(2)}) collective-permute-start(f32[8,256]{1,0:T(8,128)S(1)} %iterate.3.mid_ref), channel_id=1, source_target_pairs={{0,3},{1,0},{2,1},{3,2},{4,7},{5,4},{6,5},{7,6},{8,11},{9,8},{10,9... | collective-permute-start | bytes 24584 | tf_op jit(solution)/shard_map/ppermute | solution.py:498
  122.3 4.0 %collective-permute-start.13 = (f32[8,256]{1,0:T(8,128)S(1)}, f32[8,256]{1,0:T(8,128)S(1)}, u32[]{:S(2)}, u32[]{:S(2)}) collective-permute-start(f32[8,256]{1,0:T(8,128)S(1)} %iterate.3.mid_ref), channel_id=1, source_target_pairs={{0,1},{1,2},{2,3},{3,0},{4,5},{5,6},{6,7},{7,4},{8,9},{9,10},{10,1... | collective-permute-start | bytes 24584 | tf_op jit(solution)/shard_map/ppermute | solution.py:497
  138.9 3.9 %collective-permute-start.15 = (bf16[32,8,256]{2,1,0:T(8,128)(2,1)S(1)}, bf16[32,8,256]{2,1,0:T(8,128)(2,1)S(1)}, u32[]{:S(2)}, u32[]{:S(2)}) collective-permute-start(bf16[32,8,256]{2,1,0:T(8,128)(2,1)S(1)} %all_to_all.26), channel_id=1, source_target_pairs={{0,4},{4,0},{1,5},{5,1},{2,6},{6,2},{3,7},{7,3},{8,12},{12,8},{9,1... | collective-permute-start | bytes 393224 | tf_op jit(solution)/shard_map/ppermute | solution.py:502
  145.8 2.5 %collective-permute-start.17 = (f32[8,256]{1,0:T(8,128)S(1)}, f32[8,256]{1,0:T(8,128)S(1)}, u32[]{:S(2)}, u32[]{:S(2)}) collective-permute-start(f32[8,256]{1,0:T(8,128)S(1)} %iterate.4.mid_ref), channel_id=1, source_target_pairs={{0,3},{1,0},{2,1},{3,2},{4,7},{5,4},{6,5},{7,6},{8,11},{9,8},{10,9... | collective-permute-start | bytes 24584 | tf_op jit(solution)/shard_map/ppermute | solution.py:498
  145.8 3.8 %collective-permute-start.16 = (f32[8,256]{1,0:T(8,128)S(1)}, f32[8,256]{1,0:T(8,128)S(1)}, u32[]{:S(2)}, u32[]{:S(2)}) collective-permute-start(f32[8,256]{1,0:T(8,128)S(1)} %iterate.4.mid_ref), channel_id=1, source_target_pairs={{0,1},{1,2},{2,3},{3,0},{4,5},{5,6},{6,7},{7,4},{8,9},{9,10},{10,1... | collective-permute-start | bytes 24584 | tf_op jit(solution)/shard_map/ppermute | solution.py:497
  162.1 3.9 %collective-permute-start.18 = (bf16[32,8,256]{2,1,0:T(8,128)(2,1)S(1)}, bf16[32,8,256]{2,1,0:T(8,128)(2,1)S(1)}, u32[]{:S(2)}, u32[]{:S(2)}) collective-permute-start(bf16[32,8,256]{2,1,0:T(8,128)(2,1)S(1)} %all_to_all.27), channel_id=1, source_target_pairs={{0,4},{4,0},{1,5},{5,1},{2,6},{6,2},{3,7},{7,3},{8,12},{12,8},{9,1... | collective-permute-start | bytes 393224 | tf_op jit(solution)/shard_map/ppermute | solution.py:502
  168.9 2.5 %collective-permute-start.20 = (f32[8,256]{1,0:T(8,128)S(1)}, f32[8,256]{1,0:T(8,128)S(1)}, u32[]{:S(2)}, u32[]{:S(2)}) collective-permute-start(f32[8,256]{1,0:T(8,128)S(1)} %iterate.5.mid_ref), channel_id=1, source_target_pairs={{0,3},{1,0},{2,1},{3,2},{4,7},{5,4},{6,5},{7,6},{8,11},{9,8},{10,9... | collective-permute-start | bytes 24584 | tf_op jit(solution)/shard_map/ppermute | solution.py:498
  168.9 3.8 %collective-permute-start.19 = (f32[8,256]{1,0:T(8,128)S(1)}, f32[8,256]{1,0:T(8,128)S(1)}, u32[]{:S(2)}, u32[]{:S(2)}) collective-permute-start(f32[8,256]{1,0:T(8,128)S(1)} %iterate.5.mid_ref), channel_id=1, source_target_pairs={{0,1},{1,2},{2,3},{3,0},{4,5},{5,6},{6,7},{7,4},{8,9},{9,10},{10,1... | collective-permute-start | bytes 24584 | tf_op jit(solution)/shard_map/ppermute | solution.py:497
